TPU v7x, 32 devices: a whole 2x2x4 slice. The times are simulated.
32 devices in a mesh: rep: 2 (over y), req: 4 (over z), mp: 4 (over x, core).
Axes of the slice: x: 2, y: 2, z: 4, core: 2. Of those that a mesh axis runs over, the one named last changes fastest.
Arguments:
- hidden_in: bfloat16 [128, 2, 8192], P(('rep', 'req'), None, 'mp'), parts along dimension 0, may hold values from -6 to 6
- frozen_query_rows: bfloat16 [128, 2, 8192], P(('rep', 'req'), None, 'mp'), parts along dimension 0, may hold values from -6 to 86
- new_kv: bfloat16 [128, 2, 2, 1024], P(('rep', 'req'), None, None, 'mp'), parts along dimension 0, may hold values from -6 to 31
- adapter_of: int32 [128], P(('rep', 'req')), parts along dimension 0, may hold values from 0 to 7, as said below
- adapter_home: int32 [16], P('rep'), parts along dimension 0, may hold values from 0 to 7, as said below
- a_store: bfloat16 [16, 64, 8192], P(('rep', 'req'), None, 'mp'), parts along dimension 0, may hold values from -0.0625 to 0.0625
- b_store: bfloat16 [16, 64, 8192], P(('rep', 'req'), None, 'mp'), parts along dimension 0, may hold values from -0.75 to 0.75
- kv_pool: bfloat16 [2, 1024, 16, 1024], P(None, ('rep', 'req'), None, 'mp'), parts along dimension 1, may hold values from -6 to 31
- page_table: int32 [128, 8], P(('rep', 'req')), parts along dimension 0, may hold values from 0 to 127, as said below
- cached_len: int32 [128], P(('rep', 'req')), parts along dimension 0, may hold values from 32 to 128
- new_group: int32 [128], P(('rep', 'req')), parts along dimension 0, may hold values from 0 to 3, as said below
Outputs:
- attended: bfloat16 [128, 2, 8192], P(('rep', 'req'), None, 'mp'), parts along dimension 0
- cache: bfloat16 [2, 128, 128, 1024], P(None, ('rep', 'req'), None, 'mp'), parts along dimension 1
There are 2 independent parts, one for each index of `rep`. A program takes and returns all parts, laid end to end along the dimension named above; each array names one. Nothing has to cross between parts.
Inputs may be any that keep to these rules, and one draw needn't show every extreme that they name: A permutation: adapter a lives in store slot adapter_home[a], which belongs to group adapter_home[a] div 2. `adapter_of`: the requests of one group (new rows h * 16 to h * 16 + 15) use adapters of min(16, number of groups) different owners, at most 4 requests an owner, a number reached in every group; all requests of one group whose adapters have one owner use the same adapter. `page_table`: the rows of one group name each of its 128 pages once. `new_group`: A request keeps its slot (row mod 16); the same 4 slots keep their group in every group; every group receives exactly one request into each slot; no group sends more than 3 requests to one other group, and some pair of groups reaches it.
All inputs are finite; a program needn't handle non-finite values.
Results may differ from a plain program's by a relative error of at most 0.0069.
Values may be sent and summed in bfloat16 or wider, within the bound.
A program may use at most 64 MiB of HBM per device.

v0:
```python
import jax
import jax.numpy as jnp
from jax import lax
from jax.sharding import PartitionSpec as P

HEAD = 128
NEG_FILL = -1e30


def attend(query_vectors, cached_keys, cached_values, length, fresh_kv):
    row_count, step_count, q_width = query_vectors.shape
    context = cached_keys.shape[1]
    kv_width = cached_keys.shape[2]
    kv_heads = kv_width // HEAD
    per_kv = q_width // kv_width
    score_scale = HEAD ** (-0.5)
    q_split = query_vectors.reshape(row_count, step_count, kv_heads, per_kv, HEAD)
    k_split = cached_keys.reshape(row_count, context, kv_heads, HEAD)
    v_split = cached_values.reshape(row_count, context, kv_heads, HEAD)
    new_keys = fresh_kv[:, :, 0].reshape(row_count, step_count, kv_heads, HEAD)
    new_values = fresh_kv[:, :, 1].reshape(row_count, step_count, kv_heads, HEAD)
    old_scores = (
        jnp.einsum("bskgd,bjkd->bskgj", q_split, k_split, preferred_element_type=jnp.float32)
        * score_scale
    )
    visible = jnp.arange(context)[None, :] < length[:, None]
    old_scores = jnp.where(visible[:, None, None, None, :], old_scores, NEG_FILL)
    new_scores = (
        jnp.einsum("bskgd,btkd->bskgt", q_split, new_keys, preferred_element_type=jnp.float32)
        * score_scale
    )
    causal = jnp.arange(step_count)[None, :] <= jnp.arange(step_count)[:, None]
    new_scores = jnp.where(causal[None, :, None, None, :], new_scores, NEG_FILL)
    scores = jnp.concatenate([old_scores, new_scores], axis=-1)
    row_max = jnp.max(scores, axis=-1, keepdims=True)
    weights = jnp.exp(scores - row_max)
    probabilities = (weights / jnp.sum(weights, axis=-1, keepdims=True)).astype(jnp.bfloat16)
    attention_out = jnp.einsum(
        "bskgj,bjkd->bskgd",
        probabilities[..., :context],
        v_split,
        preferred_element_type=jnp.float32,
    )
    attention_out = attention_out + jnp.einsum(
        "bskgt,btkd->bskgd",
        probabilities[..., context:],
        new_values,
        preferred_element_type=jnp.float32,
    )
    return attention_out.reshape(row_count, step_count, q_width).astype(jnp.bfloat16)


def adapter_rank_width(rank_partial_sum):
    return lax.psum(rank_partial_sum, "mp")


def per_device(
    hidden_in,
    frozen_query_rows,
    new_kv,
    adapter_of,
    adapter_home,
    a_store,
    b_store,
    kv_pool,
    page_table,
    cached_len,
    new_group,
):
    groups = lax.axis_size("req")
    my_group = lax.axis_index("req")
    per_group = adapter_of.shape[0]
    store_count = a_store.shape[0]
    context = page_table.shape[1] * kv_pool.shape[2]
    kv_width = kv_pool.shape[3]
    move_cap = -(-(per_group - per_group // 4) // groups)
    group_ids = jnp.arange(groups, dtype=jnp.int32)
    slot_ids = jnp.arange(per_group, dtype=jnp.int32)
    buffer_ids = jnp.arange(groups * move_cap, dtype=jnp.int32)
    adapter_slot = jnp.take(adapter_home, adapter_of)
    owners = adapter_slot // store_count
    local_pick = adapter_slot % store_count
    owner_hit = owners[:, None] == group_ids[None, :]
    wanted = jnp.max(jnp.where(owner_hit, local_pick[:, None], -1), axis=0)
    moving = new_group != my_group
    dest_hit = (new_group[:, None] == group_ids[None, :]) & moving[:, None]
    order_in = jnp.cumsum(dest_hit.astype(jnp.int32), axis=0) - 1
    position = jnp.sum(jnp.where(dest_hit, order_in, 0), axis=1)
    flat_slot = jnp.where(moving, new_group * move_cap + position, -1)
    slot_match = flat_slot[None, :] == buffer_ids[:, None]
    send_src = jnp.where(
        jnp.any(slot_match, axis=1),
        jnp.sum(jnp.where(slot_match, slot_ids[None, :], 0), axis=1),
        -1,
    )
    safe_src = jnp.maximum(send_src, 0)
    send_len = jnp.where(send_src >= 0, jnp.take(cached_len, safe_src), 0)
    got_wanted, got_slots, got_lens = (
        lax.all_to_all(wanted, "req", split_axis=0, concat_axis=0, tiled=True),
        lax.all_to_all(
            send_src.reshape(groups, move_cap), "req", split_axis=0, concat_axis=0, tiled=True
        ),
        lax.all_to_all(
            send_len.reshape(groups, move_cap), "req", split_axis=0, concat_axis=0, tiled=True
        ),
    )
    page_rows = jnp.take(kv_pool, page_table.reshape(-1), axis=1)
    cache_old = page_rows.reshape(2, per_group, context, kv_width)
    incoming = got_slots.reshape(-1)
    in_match = incoming[None, :] == slot_ids[:, None]
    in_index = jnp.sum(jnp.where(in_match, buffer_ids[None, :], 0), axis=1)
    len_new = jnp.where(moving, jnp.take(got_lens.reshape(-1), in_index), cached_len)
    wanted_slot = jnp.maximum(got_wanted, 0)
    a_panels, b_panels = (
        lax.all_to_all(
            jnp.take(a_store, wanted_slot, axis=0), "req", split_axis=0, concat_axis=0, tiled=True
        ),
        lax.all_to_all(
            jnp.take(b_store, wanted_slot, axis=0), "req", split_axis=0, concat_axis=0, tiled=True
        ),
    )
    a_rows = jnp.take(a_panels, owners, axis=0)
    up_panel_rows = jnp.take(b_panels, owners, axis=0)
    rank_slice_product = jnp.einsum(
        "rsd,rkd->rsk", hidden_in, a_rows, preferred_element_type=jnp.float32
    )
    complete_rank_product = adapter_rank_width(rank_slice_product).astype(jnp.bfloat16)
    adapter_query_delta = jnp.einsum(
        "gxj,gjv->gxv", complete_rank_product, up_panel_rows, preferred_element_type=jnp.float32
    )
    query_vectors = (frozen_query_rows.astype(jnp.float32) + adapter_query_delta).astype(
        jnp.bfloat16
    )
    far_cache = jnp.take(cache_old, safe_src, axis=1)
    send_pages = far_cache.reshape(2, groups, move_cap, context, kv_width)
    got_pages = lax.all_to_all(send_pages, "req", split_axis=1, concat_axis=1, tiled=True)
    pooled = jnp.concatenate(
        [cache_old, got_pages.reshape(2, groups * move_cap, context, kv_width)], axis=1
    )
    source = jnp.where(moving, per_group + in_index, slot_ids)
    cache_new = jnp.take(pooled, source, axis=1)
    attended = attend(query_vectors, cache_new[0], cache_new[1], len_new, new_kv)
    return (attended, cache_new)


def solution(mesh):
    placed = (
        P(("rep", "req"), None, "mp"),
        P(("rep", "req"), None, "mp"),
        P(("rep", "req"), None, None, "mp"),
        P(("rep", "req")),
        P("rep"),
        P(("rep", "req"), None, "mp"),
        P(("rep", "req"), None, "mp"),
        P(None, ("rep", "req"), None, "mp"),
        P(("rep", "req"), None),
        P(("rep", "req")),
        P(("rep", "req")),
    )
    return jax.shard_map(
        per_device,
        mesh=mesh,
        in_specs=placed,
        out_specs=(P(("rep", "req"), None, "mp"), P(None, ("rep", "req"), None, "mp")),
        check_vma=False,
    )
```

profile of v0, /device:TPU:0, one launch (start us, length us, event | category | flops | bytes accessed | tf_op | source)
XLA Modules:
  0.0 155.8 jit_solution(11224241576532435948)
XLA Ops:
  0.6 0.8 compare_select_fusion.3
  1.5 1.3 gather_fusion.5
  2.8 0.7 compare_and_fusion.1
  3.6 0.7 copy.112
  4.2 6.3 %all-to-all-start.3 = ((s32[4,1,1]{2,1,0:T(1,128)}), s32[4,1,1]{2,1,0:T(1,128)S(1)}, u32[]{:S(2)}, u32[]{:S(2)}) async-start(s32[4,1,1]{2,1,0:T(1,128)} %copy.112), calls=%async_computation.3 | async-start | bytes 4096 | tf_op jit(solution)/shard_map/all_to_all | solution.py:99
  10.5 0.7 broadcast_compare_fusion.1
  11.2 0.7 fusion.34
  12.0 0.8 select_reduce_fusion.3
  12.8 0.7 add_select_fusion
  13.5 0.1 fusion.32
  13.7 0.7 select_n.200
  14.4 1.3 gather_fusion.3
  15.8 1.3 select_select_fusion
  17.1 5.1 %all-to-all-start = ((s32[4,1,3]{2,1,0:T(1,128)}), s32[4,1,3]{2,1,0:T(1,128)S(1)}, u32[]{:S(2)}, u32[]{:S(2)}) async-start(s32[4,1,3]{2,1,0:T(1,128)} %bitcast), calls=%async_computation | async-start | bytes 4096 | tf_op jit(solution)/shard_map/all_to_all | solution.py:100
  22.2 0.2 maximum_reduce_fusion
  22.4 1.7 %gather_fusion.6 = bf16[4,64,2048]{2,1,0:T(8,128)(2,1)S(1)} fusion(bf16[2,64,2048]{2,1,0:T(8,128)(2,1)} %param.20, s32[1024]{0:T(1024)S(1)} %pad_clamp_fusion.1), kind=kCustom, calls=%fused_computation.clone | custom fusion | bytes 2097168 | tf_op jit(solution)/shard_map/jit(_take)/gather | solution.py:116
  24.0 2.6 %gather_fusion.8 = bf16[4,64,2048]{2,1,0:T(8,128)(2,1)} fusion(bf16[2,64,2048]{2,1,0:T(8,128)(2,1)} %param.21, s32[1024]{0:T(1024)S(1)} %pad_clamp_fusion.1), kind=kCustom, calls=%fused_computation.2.clone | custom fusion | bytes 2097168 | tf_op jit(solution)/shard_map/jit(_take)/gather | solution.py:119
  26.7 1.0 all-to-all-done
  27.6 4.1 %all-to-all-start.2 = ((s32[4,1,3]{2,1,0:T(1,128)}), s32[4,1,3]{2,1,0:T(1,128)S(1)}, u32[]{:S(2)}, u32[]{:S(2)}) async-start(s32[4,1,3]{2,1,0:T(1,128)} %bitcast.10), calls=%async_computation.2 | async-start | bytes 4096 | tf_op jit(solution)/shard_map/all_to_all | solution.py:103
  31.8 2.8 %broadcast_select_fusion.1 = (bf16[4,64,2048]{2,1,0:T(8,128)(2,1)}, bf16[4,64,2048]{2,1,0:T(8,128)(2,1)}) fusion(bf16[4,64,2048]{2,1,0:T(8,128)(2,1)S(1)} %gather_fusion.6, pred[4]{0:T(512)(128)(4,1)S(1)} %compare_and_fusion.2, bf16[4,64,2048]{2,1,0:T(8,128)(2,1)} %gather_fusion.8), kind=kLoop, calls=%fused_computation.36 | loop fusion | flops 1048576 | bytes 4194308 | tf_op jit(solution)/shard_map/jit(_take)/select_n | solution.py:116
  34.6 2.6 %all-to-all-done.2 = s32[4,1,3]{2,1,0:T(1,128)S(1)} async-done(((s32[4,1,3]{2,1,0:T(1,128)}), s32[4,1,3]{2,1,0:T(1,128)S(1)}, u32[]{:S(2)}, u32[]{:S(2)}) %all-to-all-start.2) | async-done | bytes 80 | tf_op jit(solution)/shard_map/all_to_all | solution.py:103
  37.1 3.5 %all-to-all-start.4 = ((bf16[4,64,2048]{2,1,0:T(8,128)(2,1)}), bf16[4,64,2048]{2,1,0:T(8,128)(2,1)S(1)}, u32[]{:S(2)}, u32[]{:S(2)}) async-start(bf16[4,64,2048]{2,1,0:T(8,128)(2,1)} %get-tuple-element.25), calls=%async_computation.4 | async-start | bytes 2097152 | tf_op jit(solution)/shard_map/all_to_all | solution.py:115
  40.8 23.4 %all-to-all-done.4 = bf16[4,64,2048]{2,1,0:T(8,128)(2,1)S(1)} async-done(((bf16[4,64,2048]{2,1,0:T(8,128)(2,1)}), bf16[4,64,2048]{2,1,0:T(8,128)(2,1)S(1)}, u32[]{:S(2)}, u32[]{:S(2)}) %all-to-all-start.4) | async-done | bytes 1048608 | tf_op jit(solution)/shard_map/all_to_all | solution.py:115
  64.2 4.2 %all-to-all-start.5 = ((bf16[4,64,2048]{2,1,0:T(8,128)(2,1)}), bf16[4,64,2048]{2,1,0:T(8,128)(2,1)}, u32[]{:S(2)}, u32[]{:S(2)}) async-start(bf16[4,64,2048]{2,1,0:T(8,128)(2,1)} %get-tuple-element.26), calls=%async_computation.5 | async-start | bytes 2097152 | tf_op jit(solution)/shard_map/all_to_all | solution.py:118
  68.5 2.0 %gather_fusion = bf16[128,2,16,256]{3,2,1,0:T(8,128)(2,1)} fusion(bf16[2,128,16,256]{3,2,1,0:T(8,128)(2,1)S(1)} %copy-done, s32[1024]{0:T(1024)S(1)} %pad_clamp_fusion.6), kind=kCustom, calls=%fused_computation.4 | custom fusion | bytes 4194816 | tf_op jit(solution)/shard_map/jit(_take)/gather | solution.py:107
  70.5 3.1 %copy.106 = bf16[2,128,16,256]{3,2,1,0:T(8,128)(2,1)} copy(bf16[2,128,16,256]{3,2,0,1:T(8,128)(2,1)} %bitcast.52) | data formatting | bytes 4194304 | tf_op jit(solution)/shard_map/jit(_take)/gather | solution.py:107
  73.9 2.8 %bitcast_select_fusion = bf16[2,16,128,256]{3,2,1,0:T(8,128)(2,1)} fusion(pred[16,128]{1,0:T(8,128)(4,1)S(1)} %broadcast_in_dim.159, bf16[2,16,128,256]{3,2,1,0:T(8,128)(2,1)} %bitcast.51), kind=kLoop, calls=%fused_computation.19 | loop fusion | flops 1048576 | bytes 4196352 | tf_op jit(solution)/shard_map/jit(_take)/select_n | solution.py:107
  76.7 3.4 %gather_fusion.1 = bf16[12,2,128,256]{3,2,1,0:T(8,128)(2,1)} fusion(bf16[2,16,128,256]{3,2,1,0:T(8,128)(2,1)} %bitcast_select_fusion, s32[1024]{0:T(1024)S(1)} %pad_clamp_fusion.5), kind=kCustom, calls=%fused_computation.5 | custom fusion | bytes 3145776 | tf_op jit(solution)/shard_map/jit(_take)/gather | solution.py:134
  80.2 0.2 slice_reduce_fusion
  80.4 0.6 reshape.370
  81.0 2.9 %copy_select_fusion = bf16[2,4,3,128,256]{4,3,2,0,1:T(8,128)(2,1)} fusion(bf16[2,4,3,128,256]{4,3,0,2,1:T(8,128)(2,1)} %bitcast.54, pred[4,3]{1,0:T(4,128)(4,1)S(1)} %le.81), kind=kLoop, calls=%fused_computation.23 | loop fusion | flops 786432 | bytes 3145740 | tf_op jit(solution)/shard_map/jit(_take)/select_n | solution.py:134
  83.9 9.9 %all-to-all-done.5 = bf16[4,64,2048]{2,1,0:T(8,128)(2,1)} async-done(((bf16[4,64,2048]{2,1,0:T(8,128)(2,1)}), bf16[4,64,2048]{2,1,0:T(8,128)(2,1)}, u32[]{:S(2)}, u32[]{:S(2)}) %all-to-all-start.5) | async-done | bytes 1048608 | tf_op jit(solution)/shard_map/all_to_all | solution.py:118
  93.8 4.3 %all-to-all-start.1 = ((bf16[2,4,3,128,256]{4,3,2,0,1:T(8,128)(2,1)}), bf16[2,4,3,128,256]{4,3,2,0,1:T(8,128)(2,1)}, u32[]{:S(2)}, u32[]{:S(2)}) async-start(bf16[2,4,3,128,256]{4,3,2,0,1:T(8,128)(2,1)} %copy_select_fusion), calls=%async_computation.1 | async-start | bytes 3145728 | tf_op jit(solution)/shard_map/all_to_all | solution.py:136
  98.1 0.6 iota_compare_fusion.5
  98.7 0.5 broadcast.414
  99.3 0.6 reduce.14
  100.0 0.6 reduce.15
  100.8 0.7 gather_fusion.4
  101.5 0.6 compare_and_fusion.3
  102.1 0.6 pad_clamp_fusion.4
  102.7 0.7 iota_compare_fusion.1
  103.3 2.8 %gather_fusion.7 = bf16[16,64,2048]{2,1,0:T(8,128)(2,1)} fusion(bf16[4,64,2048]{2,1,0:T(8,128)(2,1)S(1)} %all-to-all-done.4, s32[1024]{0:T(1024)S(1)} %pad_clamp_fusion), kind=kCustom, calls=%fused_computation.1.clone | custom fusion | bytes 8388672 | tf_op jit(solution)/shard_map/jit(_take)/gather | solution.py:122
  106.1 4.0 %gather_fusion.9 = bf16[16,64,2048]{2,1,0:T(8,128)(2,1)} fusion(bf16[4,64,2048]{2,1,0:T(8,128)(2,1)} %all-to-all-done.5, s32[1024]{0:T(1024)S(1)} %pad_clamp_fusion), kind=kCustom, calls=%fused_computation.3.clone | custom fusion | bytes 8388672 | tf_op jit(solution)/shard_map/jit(_take)/gather | solution.py:123
  110.1 3.5 %fusion.20 = f32[16,2,64]{2,1,0:T(2,128)S(1)} fusion(bf16[16,2,2048]{2,1,0:T(2,128)(2,1)S(1)} %copy-done.9, bf16[16,64,2048]{2,1,0:T(8,128)(2,1)} %gather_fusion.7, pred[16]{0:T(512)(128)(4,1)S(1)} %get-tuple-element.16), kind=kOutput, calls=%fused_computation.34 | convolution fusion | flops 10485760 | bytes 4333584 | tf_op jit(solution)/shard_map/rsd,rkd->rsk/dot_general | solution.py:124
  113.6 10.2 %psum.7 = bf16[16,2,64]{2,1,0:T(2,128)(2,1)S(1)} all-reduce(f32[16,2,64]{2,1,0:T(2,128)S(1)} %fusion.20), channel_id=1, replica_groups=mesh['rep'=2,'req'=4,'mp'=4] {'mp'}, use_global_device_ids=true, to_apply=%region_6.9 | all-reduce | flops 2048 | bytes 12288 | tf_op jit(solution)/shard_map/psum | solution.py:54
  123.8 2.9 %fusion.9 = bf16[16,2,2048]{2,1,0:T(2,128)(2,1)S(1)} fusion(bf16[16,64,2048]{2,1,0:T(8,128)(2,1)} %gather_fusion.9, pred[16]{0:T(512)(128)(4,1)S(1)} %get-tuple-element.16, bf16[16,2,2048]{2,1,0:T(2,128)(2,1)S(1)} %copy-done.10, bf16[16,2,64]{2,1,0:T(2,128)(2,1)S(1)} %psum.7), kind=kOutput, calls=%fused_computation.18 | convolution fusion | flops 10682368 | bytes 4460560 | tf_op jit(solution)/shard_map/gxj,gjv->gxv/dot_general | solution.py:128
  126.9 0.9 fusion.42
  127.8 6.8 %all-to-all-done.1 = bf16[2,4,3,128,256]{4,3,2,0,1:T(8,128)(2,1)} async-done(((bf16[2,4,3,128,256]{4,3,2,0,1:T(8,128)(2,1)}), bf16[2,4,3,128,256]{4,3,2,0,1:T(8,128)(2,1)}, u32[]{:S(2)}, u32[]{:S(2)}) %all-to-all-start.1) | async-done | bytes 1572896 | tf_op jit(solution)/shard_map/all_to_all | solution.py:136
  134.6 1.7 %copy.108 = bf16[2,4,3,128,256]{4,3,2,1,0:T(8,128)(2,1)S(1)} copy(bf16[2,4,3,128,256]{4,3,2,0,1:T(8,128)(2,1)} %all-to-all-done.1) | data formatting | bytes 3145728 | tf_op jit(solution)/shard_map/all_to_all | solution.py:136
  136.3 0.4 copy-done.2
  136.7 2.1 %pad_maximum_fusion = bf16[2,28,128,256]{3,2,1,0:T(8,128)(2,1)} fusion(bf16[2,12,128,256]{3,2,1,0:T(8,128)(2,1)S(1)} %bitcast.53, bf16[2,16,128,256]{3,2,1,0:T(8,128)(2,1)S(1)} %copy-done.2), kind=kLoop, calls=%fused_computation.16 | loop fusion | flops 1835008 | bytes 7340032 | tf_op jit(solution)/shard_map/concatenate | solution.py:137
  138.8 4.2 %gather_fusion.2 = bf16[16,2,128,256]{3,2,1,0:T(8,128)(2,1)} fusion(bf16[2,28,128,256]{3,2,1,0:T(8,128)(2,1)} %pad_maximum_fusion, s32[1024]{0:T(1024)} %pad_clamp_fusion.4), kind=kCustom, calls=%fused_computation.6 | custom fusion | bytes 4194368 | tf_op jit(solution)/shard_map/jit(_take)/gather | solution.py:141
  143.0 1.9 %select_bitcast_fusion = bf16[2,16,128,256]{3,2,0,1:T(8,128)(2,1)S(1)} fusion(bf16[16,2,128,256]{3,2,1,0:T(8,128)(2,1)} %gather_fusion.2, pred[16]{0:T(512)(128)(4,1)S(1)} %copy-done.8), kind=kLoop, calls=%fused_computation.22 | loop fusion | flops 1048576 | bytes 4194320 | tf_op jit(solution)/shard_map/jit(_take)/select_n | solution.py:141
  144.8 1.5 fusion.40
  146.3 1.5 copy.125
  147.8 1.6 %copy.111 = bf16[1,16,128,256]{2,3,1,0:T(8,128)(2,1)S(1)} copy(bf16[1,16,128,256]{3,2,0,1:T(8,128)(2,1)} %get-tuple-element.23) | data formatting | bytes 2097152 | tf_op jit(solution)/shard_map/slice | solution.py:142
  149.4 1.2 fusion.41
  150.6 0.8 reduce_max.32
  151.4 0.3 fusion.24
  151.7 0.9 divide_convert_fusion
  152.6 1.7 %copy.109 = bf16[1,16,128,256]{2,3,1,0:T(8,128)(2,1)S(1)} copy(bf16[1,16,128,256]{3,2,0,1:T(8,128)(2,1)} %get-tuple-element.24) | data formatting | bytes 2097152 | tf_op jit(solution)/shard_map/slice | solution.py:142
  154.3 0.6 convolution_bitcast_fusion.1
  154.9 0.2 fusion.19
  155.1 0.7 reshape.372
  (56 shorter events, 1.4 us)
Async XLA Ops:
  0.6 67.9 %copy-start = (bf16[2,128,16,256]{3,2,1,0:T(8,128)(2,1)S(1)}, bf16[2,128,16,256]{3,2,1,0:T(8,128)(2,1)}, u32[]{:S(2)}) copy-start(bf16[2,128,16,256]{3,2,1,0:T(8,128)(2,1)} %param.22) | copy-start | bytes 6291460
  4.2 12.9 %all-to-all-start.3 = ((s32[4,1,1]{2,1,0:T(1,128)}), s32[4,1,1]{2,1,0:T(1,128)S(1)}, u32[]{:S(2)}, u32[]{:S(2)}) async-start(s32[4,1,1]{2,1,0:T(1,128)} %copy.112), calls=%async_computation.3 | async-start | bytes 4096 | tf_op jit(solution)/shard_map/all_to_all | solution.py:99
  17.1 10.6 %all-to-all-start = ((s32[4,1,3]{2,1,0:T(1,128)}), s32[4,1,3]{2,1,0:T(1,128)S(1)}, u32[]{:S(2)}, u32[]{:S(2)}) async-start(s32[4,1,3]{2,1,0:T(1,128)} %bitcast), calls=%async_computation | async-start | bytes 4096 | tf_op jit(solution)/shard_map/all_to_all | solution.py:100
  27.6 9.5 %all-to-all-start.2 = ((s32[4,1,3]{2,1,0:T(1,128)}), s32[4,1,3]{2,1,0:T(1,128)S(1)}, u32[]{:S(2)}, u32[]{:S(2)}) async-start(s32[4,1,3]{2,1,0:T(1,128)} %bitcast.10), calls=%async_computation.2 | async-start | bytes 4096 | tf_op jit(solution)/shard_map/all_to_all | solution.py:103
  34.6 6.1 %copy-start.5 = (s32[16,8]{0,1:T(8,128)S(1)}, s32[16,8]{0,1:T(8,128)}, u32[]{:S(2)}) copy-start(s32[16,8]{0,1:T(8,128)} %param.23) | copy-start | bytes 1540
  37.1 27.1 %all-to-all-start.4 = ((bf16[4,64,2048]{2,1,0:T(8,128)(2,1)}), bf16[4,64,2048]{2,1,0:T(8,128)(2,1)S(1)}, u32[]{:S(2)}, u32[]{:S(2)}) async-start(bf16[4,64,2048]{2,1,0:T(8,128)(2,1)} %get-tuple-element.25), calls=%async_computation.4 | async-start | bytes 2097152 | tf_op jit(solution)/shard_map/all_to_all | solution.py:115
  64.2 29.5 %all-to-all-start.5 = ((bf16[4,64,2048]{2,1,0:T(8,128)(2,1)}), bf16[4,64,2048]{2,1,0:T(8,128)(2,1)}, u32[]{:S(2)}, u32[]{:S(2)}) async-start(bf16[4,64,2048]{2,1,0:T(8,128)(2,1)} %get-tuple-element.26), calls=%async_computation.5 | async-start | bytes 2097152 | tf_op jit(solution)/shard_map/all_to_all | solution.py:118
  76.7 3.5 %copy-start.4 = (bf16[16,2,2,256]{3,2,1,0:T(2,128)(2,1)S(1)}, bf16[16,2,2,256]{3,2,1,0:T(2,128)(2,1)}, u32[]{:S(2)}) copy-start(bf16[16,2,2,256]{3,2,1,0:T(2,128)(2,1)} %param.17) | copy-start | bytes 98308
  83.9 17.6 %copy-start.7 = (s32[16]{0:T(128)S(1)}, s32[16]{0:T(128)}, u32[]{:S(2)}) copy-start(s32[16]{0:T(128)} %param.25) | copy-start | bytes 196
  83.9 18.8 %copy-start.1 = (s32[16]{0:T(128)S(1)}, s32[16]{0:T(128)}, u32[]{:S(2)}) copy-start(s32[16]{0:T(128)} %param.24) | copy-start | bytes 196
  93.8 40.9 %all-to-all-start.1 = ((bf16[2,4,3,128,256]{4,3,2,0,1:T(8,128)(2,1)}), bf16[2,4,3,128,256]{4,3,2,0,1:T(8,128)(2,1)}, u32[]{:S(2)}, u32[]{:S(2)}) async-start(bf16[2,4,3,128,256]{4,3,2,0,1:T(8,128)(2,1)} %copy_select_fusion), calls=%async_computation.1 | async-start | bytes 3145728 | tf_op jit(solution)/shard_map/all_to_all | solution.py:136
  106.1 4.0 %copy-start.9 = (bf16[16,2,2048]{2,1,0:T(2,128)(2,1)S(1)}, bf16[16,2,2048]{2,1,0:T(2,128)(2,1)}, u32[]{:S(2)}) copy-start(bf16[16,2,2048]{2,1,0:T(2,128)(2,1)} %param.15) | copy-start | bytes 393220
  110.1 13.7 %copy-start.10 = (bf16[16,2,2048]{2,1,0:T(2,128)(2,1)S(1)}, bf16[16,2,2048]{2,1,0:T(2,128)(2,1)}, u32[]{:S(2)}) copy-start(bf16[16,2,2048]{2,1,0:T(2,128)(2,1)} %param.16) | copy-start | bytes 393220
  123.8 3.1 %copy-start.6 = (bf16[16,2,2,128]{3,2,1,0:T(2,128)(2,1)S(1)}, bf16[16,2,2,128]{3,2,1,0:T(2,128)(2,1)}, u32[]{:S(2)}) copy-start(bf16[16,2,2,128]{3,2,1,0:T(2,128)(2,1)} %reshape.370) | copy-start | bytes 49156
  123.8 3.1 %copy-start.11 = (pred[2,2]{1,0:T(4,128)(4,1)S(1)}, pred[2,2]{1,0:T(4,128)(4,1)}, u32[]{:S(2)}) copy-start(pred[2,2]{1,0:T(4,128)(4,1)} %iota_compare_fusion.5) | copy-start | bytes 16
  134.6 2.1 %copy-start.2 = (bf16[2,16,128,256]{3,2,1,0:T(8,128)(2,1)S(1)}, bf16[2,16,128,256]{3,2,1,0:T(8,128)(2,1)}, u32[]{:S(2)}) copy-start(bf16[2,16,128,256]{3,2,1,0:T(8,128)(2,1)} %bitcast_select_fusion) | copy-start | bytes 6291460
  138.8 4.2 %copy-start.8 = (pred[16]{0:T(512)(128)(4,1)S(1)}, pred[16]{0:T(512)(128)(4,1)}, u32[]{:S(2)}) copy-start(pred[16]{0:T(512)(128)(4,1)} %get-tuple-element.19) | copy-start | bytes 52
  152.6 1.7 %copy-start.3 = (bf16[16,2,2,8,130]{4,3,1,2,0:T(8,128)(2,1)S(1)}, bf16[16,2,2,8,130]{4,3,1,2,0:T(8,128)(2,1)}, u32[]{:S(2)}) copy-start(bf16[16,2,2,8,130]{4,3,1,2,0:T(8,128)(2,1)} %divide_convert_fusion) | copy-start | bytes 399364
where the time goes:
time: 157 us; the launch traced here: 156 us
  waiting for transfers between devices  43.7 us (28%)
  local copies, waits for them, and re-layouts  39.6 us (25%)
  starting transfers between devices  27.6 us (18%)
  other arithmetic  24.5 us (16%)
  blocking collectives  10.2 us (6%)
  matrix products  9.32 us (6%)
    all_to_all x1, waiting for transfers between devices, per_device(): lax.all_to_all(jnp.take(a_store, wanted_slot, axis=0), 'req', split_axis=...  23.4 us
    psum x1, blocking collectives, adapter_rank_width(): return lax.psum(rank_partial_sum, 'mp')  10.2 us
    all_to_all x1, waiting for transfers between devices, per_device(): lax.all_to_all(jnp.take(b_store, wanted_slot, axis=0), 'req', split_axis=...  9.87 us
    all_to_all x1, waiting for transfers between devices, per_device(): lax.all_to_all(send_pages, 'req', split_axis=1, concat_axis=1, tiled=True)  6.84 us
    all_to_all x1, starting transfers between devices, per_device(): lax.all_to_all(wanted, 'req', split_axis=0, concat_axis=0, tiled=True)  6.32 us
    gather x2, local copies, waits for them, and re-layouts, per_device(): page_rows = jnp.take(kv_pool, page_table.reshape(-1), axis=1)  5.1 us
    all_to_all x1, starting transfers between devices, per_device(): lax.all_to_all(send_src.reshape(groups, move_cap), 'req', split_axis=0, c...  5.09 us
    all_to_all x1, starting transfers between devices, per_device(): lax.all_to_all(send_pages, 'req', split_axis=1, concat_axis=1, tiled=True)  4.35 us
  transfers between devices with their start and end apart: 6, of which 5 were waited for; matrix products, arithmetic and copies ran while one was open for 31% of the time, Pallas kernels for 0%

commit v1 on v0

--- a/solution.py
+++ b/solution.py
@@ -5,6 +5,11 @@
 
 HEAD = 128
 NEG_FILL = -1e30
+
+
+def prepare_numbers_on(mesh_ax, sample):
+    outer = lax.all_gather(sample, mesh_ax).sum(axis=0)
+    return outer
 
 
 def attend(query_vectors, cached_keys, cached_values, length, fresh_kv):
@@ -51,7 +56,7 @@
 
 
 def adapter_rank_width(rank_partial_sum):
-    return lax.psum(rank_partial_sum, "mp")
+    return prepare_numbers_on("mp", rank_partial_sum)
 
 
 def per_device(

time: 157 us -> 157 us (level)
  waiting for transfers between devices: 43.7 us -> 49 us
  blocking collectives: 10.2 us -> 5.25 us
    psum x1 -> x0, blocking collectives: 10.2 us -> none  [adapter_rank_width(): return lax.psum(rank_partial_sum, 'mp')]
    all_gather x0 -> x1, blocking collectives: none -> 5.25 us  [prepare_numbers_on(): outer = lax.all_gather(sample, mesh_ax).sum(axis=0)]
    all_to_all x1, waiting for transfers between devices: 6.84 us -> 12.1 us  [per_device(): lax.all_to_all(send_pages, 'req', split_axis=1, concat_axis=1, tiled=True)]
where the time goes in v1:
time: 157 us; the launch traced here: 156 us
  waiting for transfers between devices  49 us (31%)
  local copies, waits for them, and re-layouts  39.5 us (25%)
  starting transfers between devices  27.6 us (18%)
  other arithmetic  24.3 us (15%)
  matrix products  9.27 us (6%)
  blocking collectives  5.25 us (3%)
    all_to_all x1, waiting for transfers between devices, per_device(): lax.all_to_all(jnp.take(a_store, wanted_slot, axis=0), 'req', split_axis=...  23.4 us
    all_to_all x1, waiting for transfers between devices, per_device(): lax.all_to_all(send_pages, 'req', split_axis=1, concat_axis=1, tiled=True)  12.1 us
    all_to_all x1, waiting for transfers between devices, per_device(): lax.all_to_all(jnp.take(b_store, wanted_slot, axis=0), 'req', split_axis=...  9.93 us
    all_to_all x1, starting transfers between devices, per_device(): lax.all_to_all(wanted, 'req', split_axis=0, concat_axis=0, tiled=True)  6.32 us
    all_gather x1, blocking collectives, prepare_numbers_on(): outer = lax.all_gather(sample, mesh_ax).sum(axis=0)  5.25 us
    gather x2, local copies, waits for them, and re-layouts, per_device(): page_rows = jnp.take(kv_pool, page_table.reshape(-1), axis=1)  5.1 us
    all_to_all x1, starting transfers between devices, per_device(): lax.all_to_all(send_src.reshape(groups, move_cap), 'req', split_axis=0, c...  5.09 us
    all_to_all x1, starting transfers between devices, per_device(): lax.all_to_all(send_pages, 'req', split_axis=1, concat_axis=1, tiled=True)  4.34 us
  transfers between devices with their start and end apart: 6, of which 5 were waited for; matrix products, arithmetic and copies ran while one was open for 31% of the time, Pallas kernels for 0%

profile of v1, /device:TPU:0, one launch (start us, length us, event | category | flops | bytes accessed | tf_op | source)
XLA Modules:
  0.0 155.8 jit_solution(5423815510068550758)
XLA Ops:
  0.6 0.8 compare_select_fusion.3
  1.5 1.3 gather_fusion.5
  2.8 0.7 compare_and_fusion.1
  3.6 0.7 copy.112
  4.2 6.3 %all-to-all-start.3 = ((s32[4,1,1]{2,1,0:T(1,128)}), s32[4,1,1]{2,1,0:T(1,128)S(1)}, u32[]{:S(2)}, u32[]{:S(2)}) async-start(s32[4,1,1]{2,1,0:T(1,128)} %copy.112), calls=%async_computation.3 | async-start | bytes 4096 | tf_op jit(solution)/shard_map/all_to_all | solution.py:104
  10.5 0.7 broadcast_compare_fusion.1
  11.2 0.7 fusion.34
  12.0 0.8 select_reduce_fusion.3
  12.8 0.7 add_select_fusion
  13.5 0.1 fusion.32
  13.7 0.7 select_n.200
  14.4 1.3 gather_fusion.3
  15.8 1.3 select_select_fusion
  17.1 5.1 %all-to-all-start = ((s32[4,1,3]{2,1,0:T(1,128)}), s32[4,1,3]{2,1,0:T(1,128)S(1)}, u32[]{:S(2)}, u32[]{:S(2)}) async-start(s32[4,1,3]{2,1,0:T(1,128)} %bitcast), calls=%async_computation | async-start | bytes 4096 | tf_op jit(solution)/shard_map/all_to_all | solution.py:105
  22.2 0.2 maximum_reduce_fusion
  22.4 1.7 %gather_fusion.6 = bf16[4,64,2048]{2,1,0:T(8,128)(2,1)S(1)} fusion(bf16[2,64,2048]{2,1,0:T(8,128)(2,1)} %param.20, s32[1024]{0:T(1024)S(1)} %pad_clamp_fusion.1), kind=kCustom, calls=%fused_computation.clone | custom fusion | bytes 2097168 | tf_op jit(solution)/shard_map/jit(_take)/gather | solution.py:121
  24.0 2.6 %gather_fusion.8 = bf16[4,64,2048]{2,1,0:T(8,128)(2,1)} fusion(bf16[2,64,2048]{2,1,0:T(8,128)(2,1)} %param.21, s32[1024]{0:T(1024)S(1)} %pad_clamp_fusion.1), kind=kCustom, calls=%fused_computation.2.clone | custom fusion | bytes 2097168 | tf_op jit(solution)/shard_map/jit(_take)/gather | solution.py:124
  26.7 1.0 all-to-all-done
  27.6 4.1 %all-to-all-start.2 = ((s32[4,1,3]{2,1,0:T(1,128)}), s32[4,1,3]{2,1,0:T(1,128)S(1)}, u32[]{:S(2)}, u32[]{:S(2)}) async-start(s32[4,1,3]{2,1,0:T(1,128)} %bitcast.10), calls=%async_computation.2 | async-start | bytes 4096 | tf_op jit(solution)/shard_map/all_to_all | solution.py:108
  31.8 2.8 %broadcast_select_fusion.1 = (bf16[4,64,2048]{2,1,0:T(8,128)(2,1)}, bf16[4,64,2048]{2,1,0:T(8,128)(2,1)}) fusion(bf16[4,64,2048]{2,1,0:T(8,128)(2,1)S(1)} %gather_fusion.6, pred[4]{0:T(512)(128)(4,1)S(1)} %compare_and_fusion.2, bf16[4,64,2048]{2,1,0:T(8,128)(2,1)} %gather_fusion.8), kind=kLoop, calls=%fused_computation.36 | loop fusion | flops 1048576 | bytes 4194308 | tf_op jit(solution)/shard_map/jit(_take)/select_n | solution.py:121
  34.6 2.6 %all-to-all-done.2 = s32[4,1,3]{2,1,0:T(1,128)S(1)} async-done(((s32[4,1,3]{2,1,0:T(1,128)}), s32[4,1,3]{2,1,0:T(1,128)S(1)}, u32[]{:S(2)}, u32[]{:S(2)}) %all-to-all-start.2) | async-done | bytes 80 | tf_op jit(solution)/shard_map/all_to_all | solution.py:108
  37.1 3.5 %all-to-all-start.4 = ((bf16[4,64,2048]{2,1,0:T(8,128)(2,1)}), bf16[4,64,2048]{2,1,0:T(8,128)(2,1)S(1)}, u32[]{:S(2)}, u32[]{:S(2)}) async-start(bf16[4,64,2048]{2,1,0:T(8,128)(2,1)} %get-tuple-element.25), calls=%async_computation.4 | async-start | bytes 2097152 | tf_op jit(solution)/shard_map/all_to_all | solution.py:120
  40.8 23.4 %all-to-all-done.4 = bf16[4,64,2048]{2,1,0:T(8,128)(2,1)S(1)} async-done(((bf16[4,64,2048]{2,1,0:T(8,128)(2,1)}), bf16[4,64,2048]{2,1,0:T(8,128)(2,1)S(1)}, u32[]{:S(2)}, u32[]{:S(2)}) %all-to-all-start.4) | async-done | bytes 1048608 | tf_op jit(solution)/shard_map/all_to_all | solution.py:120
  64.2 4.2 %all-to-all-start.5 = ((bf16[4,64,2048]{2,1,0:T(8,128)(2,1)}), bf16[4,64,2048]{2,1,0:T(8,128)(2,1)}, u32[]{:S(2)}, u32[]{:S(2)}) async-start(bf16[4,64,2048]{2,1,0:T(8,128)(2,1)} %get-tuple-element.26), calls=%async_computation.5 | async-start | bytes 2097152 | tf_op jit(solution)/shard_map/all_to_all | solution.py:123
  68.5 2.0 %gather_fusion = bf16[128,2,16,256]{3,2,1,0:T(8,128)(2,1)} fusion(bf16[2,128,16,256]{3,2,1,0:T(8,128)(2,1)S(1)} %copy-done, s32[1024]{0:T(1024)S(1)} %pad_clamp_fusion.6), kind=kCustom, calls=%fused_computation.4 | custom fusion | bytes 4194816 | tf_op jit(solution)/shard_map/jit(_take)/gather | solution.py:112
  70.5 3.1 %copy.106 = bf16[2,128,16,256]{3,2,1,0:T(8,128)(2,1)} copy(bf16[2,128,16,256]{3,2,0,1:T(8,128)(2,1)} %bitcast.53) | data formatting | bytes 4194304 | tf_op jit(solution)/shard_map/jit(_take)/gather | solution.py:112
  73.9 2.8 %bitcast_select_fusion = bf16[2,16,128,256]{3,2,1,0:T(8,128)(2,1)} fusion(pred[16,128]{1,0:T(8,128)(4,1)S(1)} %broadcast_in_dim.159, bf16[2,16,128,256]{3,2,1,0:T(8,128)(2,1)} %bitcast.52), kind=kLoop, calls=%fused_computation.19 | loop fusion | flops 1048576 | bytes 4196352 | tf_op jit(solution)/shard_map/jit(_take)/select_n | solution.py:112
  76.7 3.4 %gather_fusion.1 = bf16[12,2,128,256]{3,2,1,0:T(8,128)(2,1)} fusion(bf16[2,16,128,256]{3,2,1,0:T(8,128)(2,1)} %bitcast_select_fusion, s32[1024]{0:T(1024)S(1)} %pad_clamp_fusion.5), kind=kCustom, calls=%fused_computation.5 | custom fusion | bytes 3145776 | tf_op jit(solution)/shard_map/jit(_take)/gather | solution.py:139
  80.2 0.2 slice_reduce_fusion
  80.4 0.6 reshape.371
  81.0 2.8 %copy_select_fusion = bf16[2,4,3,128,256]{4,3,2,0,1:T(8,128)(2,1)} fusion(bf16[2,4,3,128,256]{4,3,0,2,1:T(8,128)(2,1)} %bitcast.55, pred[4,3]{1,0:T(4,128)(4,1)S(1)} %le.81), kind=kLoop, calls=%fused_computation.23 | loop fusion | flops 786432 | bytes 3145740 | tf_op jit(solution)/shard_map/jit(_take)/select_n | solution.py:139
  83.8 9.9 %all-to-all-done.5 = bf16[4,64,2048]{2,1,0:T(8,128)(2,1)} async-done(((bf16[4,64,2048]{2,1,0:T(8,128)(2,1)}), bf16[4,64,2048]{2,1,0:T(8,128)(2,1)}, u32[]{:S(2)}, u32[]{:S(2)}) %all-to-all-start.5) | async-done | bytes 1048608 | tf_op jit(solution)/shard_map/all_to_all | solution.py:123
  93.8 4.3 %all-to-all-start.1 = ((bf16[2,4,3,128,256]{4,3,2,0,1:T(8,128)(2,1)}), bf16[2,4,3,128,256]{4,3,2,0,1:T(8,128)(2,1)}, u32[]{:S(2)}, u32[]{:S(2)}) async-start(bf16[2,4,3,128,256]{4,3,2,0,1:T(8,128)(2,1)} %copy_select_fusion), calls=%async_computation.1 | async-start | bytes 3145728 | tf_op jit(solution)/shard_map/all_to_all | solution.py:141
  98.1 0.5 iota_compare_fusion.5
  98.7 0.5 broadcast.414
  99.1 0.6 reduce.14
  99.8 0.6 reduce.15
  100.6 0.7 gather_fusion.4
  101.3 0.5 compare_and_fusion.3
  101.8 0.6 pad_clamp_fusion.4
  102.4 0.7 iota_compare_fusion.1
  103.1 2.7 %gather_fusion.7 = bf16[16,64,2048]{2,1,0:T(8,128)(2,1)} fusion(bf16[4,64,2048]{2,1,0:T(8,128)(2,1)S(1)} %all-to-all-done.4, s32[1024]{0:T(1024)S(1)} %pad_clamp_fusion), kind=kCustom, calls=%fused_computation.1.clone | custom fusion | bytes 8388672 | tf_op jit(solution)/shard_map/jit(_take)/gather | solution.py:127
  105.8 3.4 %fusion.20 = f32[16,2,64]{2,1,0:T(2,128)S(1)} fusion(bf16[16,2,2048]{2,1,0:T(2,128)(2,1)S(1)} %copy-done.9, bf16[16,64,2048]{2,1,0:T(8,128)(2,1)} %gather_fusion.7, pred[16]{0:T(512)(128)(4,1)S(1)} %get-tuple-element.16), kind=kOutput, calls=%fused_computation.34 | convolution fusion | flops 10485760 | bytes 4333584 | tf_op jit(solution)/shard_map/rsd,rkd->rsk/dot_general | solution.py:129
  109.3 5.2 %all-gather = f32[64,2,64]{2,1,0:T(2,128)S(1)} all-gather(f32[16,2,64]{2,1,0:T(2,128)S(1)} %fusion.20), channel_id=2, replica_groups=mesh['rep'=2,'req'=4,'mp'=4] {'mp'}, dimensions={0}, use_global_device_ids=true | all-gather | bytes 40960 | tf_op jit(solution)/shard_map/all_gather | solution.py:11
  114.6 4.0 %gather_fusion.9 = bf16[16,64,2048]{2,1,0:T(8,128)(2,1)} fusion(bf16[4,64,2048]{2,1,0:T(8,128)(2,1)} %all-to-all-done.5, s32[1024]{0:T(1024)S(1)} %pad_clamp_fusion), kind=kCustom, calls=%fused_computation.3.clone | custom fusion | bytes 8388672 | tf_op jit(solution)/shard_map/jit(_take)/gather | solution.py:128
  118.6 3.0 %fusion.9 = bf16[16,2,2048]{2,1,0:T(2,128)(2,1)S(1)} fusion(bf16[16,64,2048]{2,1,0:T(8,128)(2,1)} %gather_fusion.9, pred[16]{0:T(512)(128)(4,1)S(1)} %get-tuple-element.16, bf16[16,2,2048]{2,1,0:T(2,128)(2,1)S(1)} %copy-done.10, bf16[16,2,64]{2,1,0:T(2,128)(2,1)S(1)} %reduce_sum.51), kind=kOutput, calls=%fused_computation.18 | convolution fusion | flops 10682368 | bytes 4460560 | tf_op jit(solution)/shard_map/gxj,gjv->gxv/dot_general | solution.py:133
  121.6 0.9 fusion.42
  122.6 12.1 %all-to-all-done.1 = bf16[2,4,3,128,256]{4,3,2,0,1:T(8,128)(2,1)} async-done(((bf16[2,4,3,128,256]{4,3,2,0,1:T(8,128)(2,1)}), bf16[2,4,3,128,256]{4,3,2,0,1:T(8,128)(2,1)}, u32[]{:S(2)}, u32[]{:S(2)}) %all-to-all-start.1) | async-done | bytes 1572896 | tf_op jit(solution)/shard_map/all_to_all | solution.py:141
  134.6 1.7 %copy.108 = bf16[2,4,3,128,256]{4,3,2,1,0:T(8,128)(2,1)S(1)} copy(bf16[2,4,3,128,256]{4,3,2,0,1:T(8,128)(2,1)} %all-to-all-done.1) | data formatting | bytes 3145728 | tf_op jit(solution)/shard_map/all_to_all | solution.py:141
  136.3 0.4 copy-done.2
  136.7 2.1 %pad_maximum_fusion = bf16[2,28,128,256]{3,2,1,0:T(8,128)(2,1)} fusion(bf16[2,12,128,256]{3,2,1,0:T(8,128)(2,1)S(1)} %bitcast.54, bf16[2,16,128,256]{3,2,1,0:T(8,128)(2,1)S(1)} %copy-done.2), kind=kLoop, calls=%fused_computation.16 | loop fusion | flops 1835008 | bytes 7340032 | tf_op jit(solution)/shard_map/concatenate | solution.py:142
  138.8 4.2 %gather_fusion.2 = bf16[16,2,128,256]{3,2,1,0:T(8,128)(2,1)} fusion(bf16[2,28,128,256]{3,2,1,0:T(8,128)(2,1)} %pad_maximum_fusion, s32[1024]{0:T(1024)} %pad_clamp_fusion.4), kind=kCustom, calls=%fused_computation.6 | custom fusion | bytes 4194368 | tf_op jit(solution)/shard_map/jit(_take)/gather | solution.py:146
  143.0 1.9 %select_bitcast_fusion = bf16[2,16,128,256]{3,2,0,1:T(8,128)(2,1)S(1)} fusion(bf16[16,2,128,256]{3,2,1,0:T(8,128)(2,1)} %gather_fusion.2, pred[16]{0:T(512)(128)(4,1)S(1)} %copy-done.8), kind=kLoop, calls=%fused_computation.22 | loop fusion | flops 1048576 | bytes 4194320 | tf_op jit(solution)/shard_map/jit(_take)/select_n | solution.py:146
  144.8 1.5 fusion.40
  146.3 1.5 copy.125
  147.8 1.6 %copy.111 = bf16[1,16,128,256]{2,3,1,0:T(8,128)(2,1)S(1)} copy(bf16[1,16,128,256]{3,2,0,1:T(8,128)(2,1)} %get-tuple-element.23) | data formatting | bytes 2097152 | tf_op jit(solution)/shard_map/slice | solution.py:147
  149.4 1.2 fusion.41
  150.6 0.8 reduce_max.32
  151.4 0.3 fusion.24
  151.7 0.9 divide_convert_fusion
  152.6 1.7 %copy.109 = bf16[1,16,128,256]{2,3,1,0:T(8,128)(2,1)S(1)} copy(bf16[1,16,128,256]{3,2,0,1:T(8,128)(2,1)} %get-tuple-element.24) | data formatting | bytes 2097152 | tf_op jit(solution)/shard_map/slice | solution.py:147
  154.3 0.6 convolution_bitcast_fusion.1
  154.9 0.2 fusion.19
  155.1 0.7 reshape.373
  (57 shorter events, 1.4 us)
Async XLA Ops:
  0.6 67.9 %copy-start = (bf16[2,128,16,256]{3,2,1,0:T(8,128)(2,1)S(1)}, bf16[2,128,16,256]{3,2,1,0:T(8,128)(2,1)}, u32[]{:S(2)}) copy-start(bf16[2,128,16,256]{3,2,1,0:T(8,128)(2,1)} %param.22) | copy-start | bytes 6291460
  4.2 12.9 %all-to-all-start.3 = ((s32[4,1,1]{2,1,0:T(1,128)}), s32[4,1,1]{2,1,0:T(1,128)S(1)}, u32[]{:S(2)}, u32[]{:S(2)}) async-start(s32[4,1,1]{2,1,0:T(1,128)} %copy.112), calls=%async_computation.3 | async-start | bytes 4096 | tf_op jit(solution)/shard_map/all_to_all | solution.py:104
  17.1 10.6 %all-to-all-start = ((s32[4,1,3]{2,1,0:T(1,128)}), s32[4,1,3]{2,1,0:T(1,128)S(1)}, u32[]{:S(2)}, u32[]{:S(2)}) async-start(s32[4,1,3]{2,1,0:T(1,128)} %bitcast), calls=%async_computation | async-start | bytes 4096 | tf_op jit(solution)/shard_map/all_to_all | solution.py:105
  27.6 9.5 %all-to-all-start.2 = ((s32[4,1,3]{2,1,0:T(1,128)}), s32[4,1,3]{2,1,0:T(1,128)S(1)}, u32[]{:S(2)}, u32[]{:S(2)}) async-start(s32[4,1,3]{2,1,0:T(1,128)} %bitcast.10), calls=%async_computation.2 | async-start | bytes 4096 | tf_op jit(solution)/shard_map/all_to_all | solution.py:108
  34.6 6.1 %copy-start.5 = (s32[16,8]{0,1:T(8,128)S(1)}, s32[16,8]{0,1:T(8,128)}, u32[]{:S(2)}) copy-start(s32[16,8]{0,1:T(8,128)} %param.23) | copy-start | bytes 1540
  37.1 27.1 %all-to-all-start.4 = ((bf16[4,64,2048]{2,1,0:T(8,128)(2,1)}), bf16[4,64,2048]{2,1,0:T(8,128)(2,1)S(1)}, u32[]{:S(2)}, u32[]{:S(2)}) async-start(bf16[4,64,2048]{2,1,0:T(8,128)(2,1)} %get-tuple-element.25), calls=%async_computation.4 | async-start | bytes 2097152 | tf_op jit(solution)/shard_map/all_to_all | solution.py:120
  64.2 29.5 %all-to-all-start.5 = ((bf16[4,64,2048]{2,1,0:T(8,128)(2,1)}), bf16[4,64,2048]{2,1,0:T(8,128)(2,1)}, u32[]{:S(2)}, u32[]{:S(2)}) async-start(bf16[4,64,2048]{2,1,0:T(8,128)(2,1)} %get-tuple-element.26), calls=%async_computation.5 | async-start | bytes 2097152 | tf_op jit(solution)/shard_map/all_to_all | solution.py:123
  76.7 3.5 %copy-start.4 = (bf16[16,2,2,256]{3,2,1,0:T(2,128)(2,1)S(1)}, bf16[16,2,2,256]{3,2,1,0:T(2,128)(2,1)}, u32[]{:S(2)}) copy-start(bf16[16,2,2,256]{3,2,1,0:T(2,128)(2,1)} %param.17) | copy-start | bytes 98308
  83.8 17.4 %copy-start.7 = (s32[16]{0:T(128)S(1)}, s32[16]{0:T(128)}, u32[]{:S(2)}) copy-start(s32[16]{0:T(128)} %param.25) | copy-start | bytes 196
  83.8 18.6 %copy-start.1 = (s32[16]{0:T(128)S(1)}, s32[16]{0:T(128)}, u32[]{:S(2)}) copy-start(s32[16]{0:T(128)} %param.24) | copy-start | bytes 196
  93.8 40.9 %all-to-all-start.1 = ((bf16[2,4,3,128,256]{4,3,2,0,1:T(8,128)(2,1)}), bf16[2,4,3,128,256]{4,3,2,0,1:T(8,128)(2,1)}, u32[]{:S(2)}, u32[]{:S(2)}) async-start(bf16[2,4,3,128,256]{4,3,2,0,1:T(8,128)(2,1)} %copy_select_fusion), calls=%async_computation.1 | async-start | bytes 3145728 | tf_op jit(solution)/shard_map/all_to_all | solution.py:141
  103.1 2.7 %copy-start.9 = (bf16[16,2,2048]{2,1,0:T(2,128)(2,1)S(1)}, bf16[16,2,2048]{2,1,0:T(2,128)(2,1)}, u32[]{:S(2)}) copy-start(bf16[16,2,2048]{2,1,0:T(2,128)(2,1)} %param.15) | copy-start | bytes 393220
  114.6 4.0 %copy-start.10 = (bf16[16,2,2048]{2,1,0:T(2,128)(2,1)S(1)}, bf16[16,2,2048]{2,1,0:T(2,128)(2,1)}, u32[]{:S(2)}) copy-start(bf16[16,2,2048]{2,1,0:T(2,128)(2,1)} %param.16) | copy-start | bytes 393220
  118.6 3.1 %copy-start.6 = (bf16[16,2,2,128]{3,2,1,0:T(2,128)(2,1)S(1)}, bf16[16,2,2,128]{3,2,1,0:T(2,128)(2,1)}, u32[]{:S(2)}) copy-start(bf16[16,2,2,128]{3,2,1,0:T(2,128)(2,1)} %reshape.371) | copy-start | bytes 49156
  118.6 3.1 %copy-start.11 = (pred[2,2]{1,0:T(4,128)(4,1)S(1)}, pred[2,2]{1,0:T(4,128)(4,1)}, u32[]{:S(2)}) copy-start(pred[2,2]{1,0:T(4,128)(4,1)} %iota_compare_fusion.5) | copy-start | bytes 16
  134.6 2.1 %copy-start.2 = (bf16[2,16,128,256]{3,2,1,0:T(8,128)(2,1)S(1)}, bf16[2,16,128,256]{3,2,1,0:T(8,128)(2,1)}, u32[]{:S(2)}) copy-start(bf16[2,16,128,256]{3,2,1,0:T(8,128)(2,1)} %bitcast_select_fusion) | copy-start | bytes 6291460
  138.8 4.2 %copy-start.8 = (pred[16]{0:T(512)(128)(4,1)S(1)}, pred[16]{0:T(512)(128)(4,1)}, u32[]{:S(2)}) copy-start(pred[16]{0:T(512)(128)(4,1)} %get-tuple-element.19) | copy-start | bytes 52
  152.6 1.7 %copy-start.3 = (bf16[16,2,2,8,130]{4,3,1,2,0:T(8,128)(2,1)S(1)}, bf16[16,2,2,8,130]{4,3,1,2,0:T(8,128)(2,1)}, u32[]{:S(2)}) copy-start(bf16[16,2,2,8,130]{4,3,1,2,0:T(8,128)(2,1)} %divide_convert_fusion) | copy-start | bytes 399364
